TPU v7x, 128 devices: a whole 4x4x4 slice. The times are simulated.
128 devices in a mesh: brick: 32 (over z, y, core), batch: 4 (over x).
Axes of the slice: x: 4, y: 4, z: 4, core: 2. Of those that a mesh axis runs over, the one named last changes fastest.
Arguments:
- crossings: int32 [16384, 8], P(('brick', 'batch')), may hold values from 0 to 31, all different within a row; in each aligned block of 128 rows (0 to 127, 128 to 255, ...) at most 64 rows name the same one
- lattice: int32 [3, 8, 4, 16384], P(None, None, None, ('brick', 'batch')), may hold values from 0 to 38
- offsets: float32 [3, 8, 4, 16384], P(None, None, None, ('brick', 'batch')), may hold values from 0 to 1
- target: float32 [3, 16384], P(None, ('brick', 'batch')), may hold values from 0 to 1
- planes: bfloat16 [32, 1600, 144], P('brick'), may hold values from -6 to 6
- line_factors: bfloat16 [32, 40, 144], P('brick'), may hold values from -6 to 6
- layer_one: bfloat16 [32, 144, 128], P('brick'), may hold values from -0.5 to 0.5
- layer_two: bfloat16 [32, 128, 128], P('brick'), may hold values from -0.5 to 0.5
- layer_out: bfloat16 [32, 128, 64], P('brick'), may hold values from -0.5 to 0.5
- density_head: bfloat16 [32, 128], P('brick'), may hold values from -0.5 to 0.5
- density_bias: float32 [32], P('brick'), may hold values from -2 to 1
- decoder_in: bfloat16 [64, 256], replicated, may hold values from -0.75 to 0.75
- decoder_out: bfloat16 [3, 256], replicated, may hold values from -0.375 to 0.375
Outputs:
- grad_planes: float32 [32, 1600, 144], P('brick')
- grad_lines: float32 [32, 40, 144], P('brick')
- grad_layer_one: float32 [32, 144, 128], P('brick')
- grad_layer_two: float32 [32, 128, 128], P('brick')
- grad_layer_out: float32 [32, 128, 64], P('brick')
- grad_density_head: float32 [32, 128], P('brick')
- grad_density_bias: float32 [32], P('brick')
- grad_decoder_in: float32 [64, 256], replicated
- grad_decoder_out: float32 [3, 256], replicated
- objective: float32 [], replicated
Inputs may be any that keep to these rules, and one draw needn't show every extreme that they name: `crossings`: A ray's 8 bricks are distinct. Among the rays of one device at most 64 cross any one brick, and in every draw some device has exactly 64 rays crossing one brick.
All inputs are finite; a program needn't handle non-finite values.
Results may differ from a plain program's by a relative error of at most 0.0098.
Values may be sent and summed in bfloat16 or wider, within the bound.
A program may use at most 64 MiB of HBM per device.

v0:
```python
import jax
import jax.numpy as jnp
from jax import lax
from jax.experimental import pallas as pl
from jax.experimental.pallas import tpu as pltpu
from jax.sharding import PartitionSpec as P

STEP_LENGTH = 0.1
MESH = pl.DeviceIdType.MESH
F32 = jnp.float32
BF16 = jnp.bfloat16

BRICKS = 32
BATCH = 4
RAYS = 128
CROSS = 8
CAP = 64
SLOTS = BRICKS * CAP
G = 40
VM = 144
COMP = 48
HID = 128
FEAT = 64
AUG = 80
DEC = 256
STRIPE = 5
STRIPES = 8
LOCAL = (STRIPE + 1) * G
WIDE = STRIPES * COMP
PEERS = 4
CHUNK = PEERS * 256
CHUNKS = BRICKS // PEERS
SAMPLES = BRICKS * CAP * 4
MSG = 40
HALF = FEAT // 2
UNITS = (48, 80, 80, 80)
BASES = (0, 384, 1024, 1664)
PACK = 2304
PAIRS = ((0, 1, 2), (0, 2, 1), (1, 2, 0))
VMEM_SPEC = pl.BlockSpec(memory_space=pltpu.VMEM)
SMEM_SPEC = pl.BlockSpec(memory_space=pltpu.SMEM)


def mm(a, b):
    return lax.dot_general(a, b, (((1,), (0,)), ((), ())), preferred_element_type=F32)


def nt(a, b):
    return lax.dot_general(a, b, (((1,), (1,)), ((), ())), preferred_element_type=F32)


def tn(a, b):
    return lax.dot_general(a, b, (((0,), (0,)), ((), ())), preferred_element_type=F32)


def split3(x):
    one = x.astype(BF16)
    rest = x - one.astype(F32)
    two = rest.astype(BF16)
    three = (rest - two.astype(F32)).astype(BF16)
    return one, two, three


def iota(shape, axis, kind=jnp.int32):
    return lax.broadcasted_iota(jnp.int32, shape, axis).astype(kind)


def eye(n):
    return jnp.where(iota((n, n), 0) == iota((n, n), 1), 1.0, 0.0).astype(BF16)


def sigmoid(v):
    return 0.5 * jnp.tanh(0.5 * v) + 0.5


def low_half(shape):
    return iota(shape, len(shape) - 1) < CAP


def swap(x):
    return pltpu.roll(x, CAP, 1)


def hat(x):
    return jnp.maximum(0.0, 1.0 - jnp.abs(x))


def place_rays(crossings, lattice, offsets, ray_slots, slot_cross, sent):
    named = crossings[...]
    brick_row = iota((BRICKS, RAYS), 0)
    crosses = jnp.zeros((BRICKS, RAYS), F32)
    order = jnp.zeros((BRICKS, RAYS), F32)
    for k in range(CROSS):
        hit = jnp.where(named[k : k + 1, :] == brick_row, 1.0, 0.0)
        crosses = crosses + hit
        order = order + float(k) * hit
    before = jnp.where(iota((RAYS, RAYS), 0) < iota((RAYS, RAYS), 1), 1.0, 0.0).astype(BF16)
    rank = mm(crosses.astype(BF16), before)
    rank = jnp.where(crosses > 0.0, rank, -1.0)
    lane = iota((BRICKS, SLOTS), 1)
    first = iota((BRICKS, SLOTS), 0) * CAP
    spread = jnp.where((lane >= first) & (lane < first + CAP), 1.0, 0.0).astype(BF16)
    place = (iota((RAYS, SLOTS), 1) & (CAP - 1)).astype(F32)
    chosen = jnp.where(tn(rank.astype(BF16), spread) == place, 1.0, 0.0)
    order_wide = tn(order.astype(BF16), spread)
    cross_of = jnp.sum(chosen * order_wide, axis=0, keepdims=True)
    chosen = chosen.astype(BF16)
    ray_slots[...] = chosen
    slot_cross[...] = jnp.broadcast_to(cross_of, (8, SLOTS))
    pad = jnp.zeros((2, RAYS), F32)
    rows = []
    for k in range(CROSS):
        for odd in range(2):
            for c in range(3):
                for half in range(2):
                    s = 2 * half + odd
                    rows.append(
                        lattice[c, k, s : s + 1, :].astype(F32) + offsets[c, k, s : s + 1, :]
                    )
            rows.append(pad)
    stacked = jnp.concatenate(split3(jnp.concatenate(rows, axis=0)), axis=0)
    height = CROSS * 16
    moved = mm(stacked, chosen)
    moved = moved[:height] + moved[height : 2 * height] + moved[2 * height :]
    picked = jnp.zeros((16, SLOTS), F32)
    for k in range(CROSS):
        picked = jnp.where(cross_of == float(k), moved[16 * k : 16 * k + 16], picked)
    low = low_half((8, 128))
    for tile in range(BRICKS // 2):
        x = picked[:, 128 * tile : 128 * tile + 128]
        even, odd = x[:8], x[8:]
        sent[2 * tile] = jnp.where(low, even, swap(odd))
        sent[2 * tile + 1] = jnp.where(low, swap(even), odd)


def turn_weights(
    planes,
    line_factors,
    layer_one,
    layer_two,
    layer_out,
    density_head,
    plane_t,
    line_t,
    one_t,
    two_t,
    out_t,
    out_aug,
):
    for h in range(STRIPES):
        at = STRIPE * G * h
        width = min(LOCAL, G * G - at)
        part = planes[0, :, at : at + width]
        if width < LOCAL:
            part = jnp.concatenate([part, jnp.zeros((VM, LOCAL - width), BF16)], axis=1)
        for p in range(3):
            plane_t[p, COMP * h : COMP * h + COMP, :] = part[COMP * p : COMP * p + COMP]
    turned = nt(eye(VM), line_factors[0])
    wide = jnp.concatenate([turned, turned, turned, jnp.zeros((VM, 8), F32)], axis=1)
    row, column = iota((VM, 128), 0), iota((VM, 128), 1)
    keep = (
        ((row < 48) & (column < 40))
        | ((row >= 48) & (row < 96) & (column >= 40) & (column < 80))
        | ((row >= 96) & (column >= 80) & (column < 120))
    )
    line_t[...] = jnp.where(keep, wide, 0.0).astype(BF16)
    unit = eye(HID)
    one_t[...] = nt(unit, layer_one[0]).astype(BF16)
    two_t[...] = nt(unit, layer_two[0]).astype(BF16)
    rows = [
        layer_out[0].astype(F32),
        density_head[...].astype(F32),
        jnp.zeros((AUG - FEAT - 1, HID), F32),
    ]
    both = jnp.concatenate(rows, axis=0).astype(BF16)
    out_t[...] = both
    out_aug[...] = nt(unit, both).astype(BF16)


def coordinate(positions, peers, c):
    parts = [
        positions[p, 2 * c + half : 2 * c + half + 1, :] for p in peers for half in range(2)
    ]
    return jnp.concatenate(parts, axis=1)


def stripe_weights(along, other_hat):
    stripe = jnp.floor(along * (1.0 / STRIPE))
    local = along - float(STRIPE) * stripe
    near = hat(local - iota((8, CHUNK), 0, F32))
    weights = jnp.concatenate(
        [near[i : i + 1] * other_hat for i in range(STRIPE + 1)], axis=0
    ).astype(BF16)
    return stripe, weights


def line_table(hats):
    rows = [hats[PAIRS[p][2]] for p in range(3)] + [jnp.zeros((8, CHUNK), F32)]
    return jnp.concatenate(rows, axis=0).astype(BF16)


def within_crossing(zeta, peer):
    low = low_half((1, 128))
    depths = []
    for half in range(2):
        at = 256 * peer + 128 * half
        z = zeta[:, at : at + 128]
        density = jnp.maximum(z, 0.0) + jnp.log1p(jnp.exp(-jnp.abs(z)))
        depths.append(STEP_LENGTH * density.astype(BF16).astype(F32))
    d0, d1 = depths
    r0, r1 = swap(d0), swap(d1)
    both = d0 + r0
    b0 = jnp.where(low, 0.0, r0)
    b1 = both + jnp.where(low, 0.0, r1)
    total = both + (d1 + r1)
    return (d0, d1), (b0, b1), total


def by_cross(row, cross_mask, ray_slots):
    out = nt(jnp.concatenate(split3(row * cross_mask), axis=0), ray_slots)
    return out[0:8] + out[8:16] + out[16:24]


def to_slots(table, cross_mask, ray_slots):
    out = mm(jnp.concatenate(split3(table), axis=0), ray_slots)
    out = out[0:8] + out[8:16] + out[16:24]
    return jnp.sum(out * cross_mask, axis=0, keepdims=True)


class Brick:
    def __init__(self):
        self.me = lax.axis_index("brick")
        self.z = self.me // 8
        self.y = lax.rem(self.me // 2, 4)
        self.core = lax.rem(self.me, 2)

    def peer(self, q, j, sign=1):
        dz = jnp.minimum(q, CHUNKS - 1 - q)
        dy = 2 * (1 - q // 4) + j // 2
        z = lax.rem(self.z + sign * dz + 4, 4)
        y = lax.rem(self.y + sign * dy + 4, 4)
        return (z * 4 + y) * 2 + lax.rem(self.core + j % 2, 2)


class Exchange:
    def __init__(self, me, sent, got, send_sem, recv_sem):
        self.me, self.sent, self.got = me, sent, got
        self.send_sem, self.recv_sem = send_sem, recv_sem

    def copy(self, peer, slot):
        return pltpu.make_async_remote_copy(
            src_ref=self.sent.at[peer],
            dst_ref=self.got.at[slot],
            send_sem=self.send_sem.at[peer],
            recv_sem=self.recv_sem.at[slot],
            device_id={"brick": peer},
            device_id_type=MESH,
        )

    def send(self, peer):
        self.copy(peer, self.me).start()

    def receive(self, peer):
        self.copy(peer, peer).wait_recv()

    def others(self, act):
        def one(d, carry):
            act(lax.rem(self.me + d, BRICKS))
            return carry

        lax.fori_loop(1, BRICKS, one, 0)

    def sends_done(self):
        self.others(lambda peer: self.copy(peer, self.me).wait_send())


def train(
    crossings,
    lattice,
    offsets,
    target,
    planes,
    line_factors,
    layer_one,
    layer_two,
    layer_out,
    density_head,
    bias,
    decoder_in,
    decoder_out,
    whole_out,
    decoder_sums,
    small_sums,
    pos_sent,
    pos_got,
    msg_sent,
    msg_got,
    back_sent,
    back_got,
    dec_sent,
    dec_got,
    dec_all,
    small_sent,
    small_got,
    ray_slots_ref,
    slot_cross,
    plane_t,
    line_t,
    one_t,
    two_t,
    out_t,
    out_aug,
    vm_s,
    plane_s,
    line_s,
    h1_s,
    s1_s,
    h2_s,
    s2_s,
    feat_s,
    zeta_s,
    gathered,
    acc_planes,
    acc_lines,
    acc_one,
    acc_two,
    acc_out,
    acc_bias,
    own,
    first_got,
    second,
    second_got,
    whole,
    pos_ss,
    pos_rs,
    msg_ss,
    msg_rs,
    back_ss,
    back_rs,
    dec_ss,
    dec_rs,
    all_ss,
    all_rs,
    small_ss,
    small_rs,
    sum_ss,
    sum_rs,
):
    at = Brick()
    me = at.me
    x = lax.axis_index("batch")
    x_peers = [lax.rem(x + d, BATCH) for d in range(1, BATCH)]
    barrier = pltpu.get_barrier_semaphore()

    def greet(d, carry):
        pl.semaphore_signal(
            barrier, inc=1, device_id={"brick": lax.rem(me + d, BRICKS)}, device_id_type=MESH
        )
        return carry

    lax.fori_loop(1, BRICKS, greet, 0)
    for peer in x_peers:
        pl.semaphore_signal(barrier, inc=1, device_id={"batch": peer}, device_id_type=MESH)

    pos = Exchange(me, pos_sent, pos_got, pos_ss, pos_rs)
    msg = Exchange(me, msg_sent, msg_got, msg_ss, msg_rs)
    back = Exchange(me, back_sent, back_got, back_ss, back_rs)
    dec = Exchange(me, dec_sent, dec_got, dec_ss, dec_rs)

    def send_near_first(exchange):
        def one(i, carry):
            for j in range(PEERS):
                peer = at.peer(CHUNKS - 1 - i, j, -1)

                @pl.when(peer != me)
                def _():
                    exchange.send(peer)

            return carry

        lax.fori_loop(0, CHUNKS, one, 0)

    place_rays(crossings, lattice, offsets, ray_slots_ref, slot_cross, pos_sent)
    pl.semaphore_wait(barrier, BRICKS - 1 + BATCH - 1)
    send_near_first(pos)
    pos_got[me] = pos_sent[me]
    turn_weights(
        planes,
        line_factors,
        layer_one,
        layer_two,
        layer_out,
        density_head,
        plane_t,
        line_t,
        one_t,
        two_t,
        out_t,
        out_aug,
    )
    for ref in (acc_lines, acc_one, acc_two, acc_out, acc_bias, dec_sent):
        ref[...] = jnp.zeros_like(ref)

    def forward(q, carry):
        peers = [at.peer(q, j) for j in range(PEERS)]
        for p in peers:

            @pl.when(p != me)
            def _():
                pos.receive(p)

        lanes = pl.ds(pl.multiple_of(q * CHUNK, CHUNK), CHUNK)
        coords = [coordinate(pos_got, peers, c) for c in range(3)]
        points = iota((G, CHUNK), 0, F32)
        hats = [hat(coord - points) for coord in coords]
        values = []
        for pair in range(3):
            a, b, line = PAIRS[pair]
            stripe, weights = stripe_weights(coords[a], hats[b])
            wide = mm(plane_t[pair], weights)
            value = wide[:COMP]
            for h in range(1, STRIPES):
                value = jnp.where(stripe == float(h), wide[COMP * h : COMP * h + COMP], value)
            values.append(value)
        plane_value = jnp.concatenate(values, axis=0)
        line_value = mm(line_t[...], line_table(hats))
        vm = (plane_value * line_value).astype(BF16)
        vm_s[:, lanes] = vm
        plane_s[:, lanes] = plane_value.astype(BF16)
        line_s[:, lanes] = line_value.astype(BF16)
        a1 = mm(one_t[...], vm)
        g1 = sigmoid(a1)
        v1 = a1 * g1
        h1 = v1.astype(BF16)
        h1_s[:, lanes] = h1
        s1_s[:, lanes] = (g1 + v1 * (1.0 - g1)).astype(BF16)
        a2 = mm(two_t[...], h1)
        g2 = sigmoid(a2)
        v2 = a2 * g2
        h2 = v2.astype(BF16)
        h2_s[:, lanes] = h2
        s2_s[:, lanes] = (g2 + v2 * (1.0 - g2)).astype(BF16)
        wide = mm(out_t[...], h2)
        feat = wide[:FEAT].astype(BF16)
        feat_s[:, lanes] = feat
        zeta = wide[FEAT : FEAT + 1] + bias[0]
        zeta_s[:, lanes] = jnp.broadcast_to(zeta, (8, CHUNK))
        low = low_half((HALF, 128))
        for j, p in enumerate(peers):
            depths, befores, total = within_crossing(zeta, j)
            summed = jnp.zeros((FEAT, 128), F32)
            for half in range(2):
                weight = jnp.exp(-befores[half]) * (1.0 - jnp.exp(-depths[half]))
                lane = 256 * j + 128 * half
                summed = summed + weight * feat[:, lane : lane + 128].astype(F32)
            summed = summed + swap(summed)
            folded = jnp.where(low, summed[:HALF], summed[HALF:])
            parts = [part.astype(F32) for part in split3(total)]
            rows = [folded] + parts + [jnp.zeros((MSG - HALF - 3, 128), F32)]
            msg_sent[p] = jnp.concatenate(rows, axis=0).astype(BF16)

            @pl.when(p != me)
            def _():
                msg.send(p)

        return carry

    lax.fori_loop(0, CHUNKS, forward, 0)
    msg_got[me] = msg_sent[me]

    ray_slots = ray_slots_ref[...]
    cross_mask = jnp.where(slot_cross[...] == iota((8, SLOTS), 0, F32), 1.0, 0.0)
    low = low_half((HALF, 128))
    low_row = low_half((1, 128))
    low8 = low_half((8, 128))
    msg.others(msg.receive)
    depth_rows = []
    for tile in range(BRICKS // 2):
        even, odd = msg_got[2 * tile].astype(F32), msg_got[2 * tile + 1].astype(F32)
        e, o = even[:HALF], odd[:HALF]
        lanes = slice(128 * tile, 128 * tile + 128)
        gathered[:HALF, lanes] = jnp.where(low, e, swap(o))
        gathered[HALF:, lanes] = jnp.where(low, swap(e), o)
        e = even[HALF : HALF + 1] + even[HALF + 1 : HALF + 2] + even[HALF + 2 : HALF + 3]
        o = odd[HALF : HALF + 1] + odd[HALF + 1 : HALF + 2] + odd[HALF + 2 : HALF + 3]
        depth_rows.append(jnp.where(low_row, e, o))
    depth = jnp.concatenate(depth_rows, axis=1)
    by_ray = by_cross(depth, cross_mask, ray_slots)
    running = jnp.zeros((1, RAYS), F32)
    befores = []
    for k in range(CROSS):
        befores.append(running)
        running = running + by_ray[k : k + 1]
    enter = to_slots(jnp.exp(-jnp.concatenate(befores, axis=0)), cross_mask, ray_slots)
    partials = gathered[...]
    scaled = partials * enter
    high = scaled.astype(BF16)
    rest = (scaled - high.astype(F32)).astype(BF16)
    composite = nt(jnp.concatenate([high, rest], axis=0), ray_slots)
    composite = (composite[:FEAT] + composite[FEAT:]).astype(BF16)
    decoder_pre = tn(decoder_in[...], composite)
    gate = sigmoid(decoder_pre)
    decoder_hidden = (decoder_pre * gate).astype(BF16)
    logits = mm(decoder_out[...], decoder_hidden)
    colors = sigmoid(logits)
    errors = colors - target[...]
    scale = float(RAYS * BRICKS * BATCH) ** (-0.5)
    grad_logits = (2.0 * scale * errors * colors * (1.0 - colors)).astype(BF16)
    back_decoder = tn(decoder_out[...], grad_logits)
    grad_pre = (back_decoder * (gate * (1.0 + decoder_pre * (1.0 - gate)))).astype(BF16)
    grad_composite = mm(decoder_in[...], grad_pre).astype(BF16)
    grad_slots = mm(grad_composite, ray_slots)
    along = jnp.sum(partials * grad_slots, axis=0, keepdims=True) * enter
    by_ray = by_cross(along, cross_mask, ray_slots)
    running = jnp.zeros((1, RAYS), F32)
    laters = []
    for k in reversed(range(CROSS)):
        laters.insert(0, running)
        running = running + by_ray[k : k + 1]
    later = to_slots(jnp.concatenate(laters, axis=0), cross_mask, ray_slots)
    for tile in range(BRICKS // 2):
        lanes = slice(128 * tile, 128 * tile + 128)
        top, bottom = grad_slots[:HALF, lanes], grad_slots[HALF:, lanes]
        scalars = [part.astype(F32) for part in split3(enter[:, lanes]) + split3(later[:, lanes])]
        scalars = jnp.concatenate(scalars + [jnp.zeros((2, 128), F32)], axis=0)
        turned = swap(scalars)
        rows = [jnp.where(low, top, swap(bottom)), jnp.where(low8, scalars, turned)]
        back_sent[2 * tile] = jnp.concatenate(rows, axis=0).astype(BF16)
        rows = [jnp.where(low, swap(top), bottom), jnp.where(low8, turned, scalars)]
        back_sent[2 * tile + 1] = jnp.concatenate(rows, axis=0).astype(BF16)
    send_near_first(back)
    back_got[me] = back_sent[me]

    objective = scale * jnp.sum(errors * errors)
    grad_out = nt(grad_logits, decoder_hidden)
    grad_in = nt(composite, grad_pre)
    for j in range(8):
        dec_sent[j] = grad_in[8 * j : 8 * j + 8, :128]
        dec_sent[8 + j] = grad_in[8 * j : 8 * j + 8, 128:]
    rows = [grad_out[:, :128], grad_out[:, 128:], jnp.full((2, 128), objective, F32)]
    dec_sent[16] = jnp.concatenate(rows, axis=0)
    dec.others(dec.send)
    dec_got[me] = dec_sent[me]

    def backward(i, carry):
        q = CHUNKS - 1 - i
        peers = [at.peer(q, j) for j in range(PEERS)]
        for p in peers:

            @pl.when(p != me)
            def _():
                back.receive(p)

        lanes = pl.ds(pl.multiple_of(q * CHUNK, CHUNK), CHUNK)
        zeta = zeta_s[0:1, lanes]
        feat = feat_s[:, lanes].astype(F32)
        grad_feats, grad_zetas = [], []
        for j, p in enumerate(peers):
            depths, befores, total = within_crossing(zeta, j)
            got = back_got[p].astype(F32)
            m = got[:HALF]
            turned = swap(m)
            grads = jnp.concatenate([jnp.where(low, m, turned), jnp.where(low, turned, m)], axis=0)
            enter = got[HALF : HALF + 1] + got[HALF + 1 : HALF + 2] + got[HALF + 2 : HALF + 3]
            later = got[HALF + 3 : HALF + 4] + got[HALF + 4 : HALF + 5] + got[HALF + 5 : HALF + 6]
            carried, lit = [], []
            for half in range(2):
                lane = 256 * j + 128 * half
                transmit = enter * jnp.exp(-befores[half])
                survive = jnp.exp(-depths[half])
                weight = transmit * (1.0 - survive)
                grad_weight = jnp.sum(grads * feat[:, lane : lane + 128], axis=0, keepdims=True)
                grad_feats.append(weight * grads)
                carried.append(grad_weight * weight)
                lit.append(grad_weight * transmit * survive)
            c0, c1 = carried
            r0, r1 = swap(c0), swap(c1)
            laters = (
                jnp.where(low_row, r0, 0.0) + (c1 + r1) + later,
                jnp.where(low_row, r1, 0.0) + later,
            )
            for half in range(2):
                lane = 256 * j + 128 * half
                grad_density = (STEP_LENGTH * (lit[half] - laters[half])).astype(BF16)
                gate = sigmoid(zeta[:, lane : lane + 128])
                grad_zetas.append((grad_density.astype(F32) * gate).astype(BF16).astype(F32))
        grad_zeta = jnp.concatenate(grad_zetas, axis=1)
        acc_bias[...] += jnp.full((8, 128), jnp.sum(grad_zeta), F32)
        rows = [jnp.concatenate(grad_feats, axis=1), grad_zeta]
        rows.append(jnp.zeros((AUG - FEAT - 1, CHUNK), F32))
        grad_aug = jnp.concatenate(rows, axis=0).astype(BF16)
        acc_out[...] += nt(grad_aug, h2_s[:, lanes])
        grad_a2 = (mm(out_aug[...], grad_aug) * s2_s[:, lanes].astype(F32)).astype(BF16)
        acc_two[...] += nt(h1_s[:, lanes], grad_a2)
        grad_a1 = (mm(layer_two[0], grad_a2) * s1_s[:, lanes].astype(F32)).astype(BF16)
        acc_one[...] += nt(vm_s[:, lanes], grad_a1)
        grad_vm = mm(layer_one[0], grad_a1)
        grad_line = (grad_vm * plane_s[:, lanes].astype(F32)).astype(BF16)
        line_s[:, lanes] = (grad_vm * line_s[:, lanes].astype(F32)).astype(BF16)
        points = iota((G, CHUNK), 0, F32)
        hats = [hat(coordinate(pos_got, peers, c) - points) for c in range(3)]
        acc_lines[...] += nt(grad_line, line_table(hats))
        return carry

    lax.fori_loop(0, CHUNKS, backward, 0)

    partner_a = x + 1 - 2 * lax.rem(x, 2)
    partner_b = BATCH - 1 - x
    keep_a = lax.rem((x + 1) // 2, 2)
    keep_b = x // 2
    partners = (partner_a, partner_b)
    keeps = (keep_a, keep_b)

    def across(src, dst, stage, step, side, partner):
        n = (stage * 4 + step) * 2 + side
        return pltpu.make_async_remote_copy(
            src_ref=src,
            dst_ref=dst,
            send_sem=sum_ss.at[n],
            recv_sem=sum_rs.at[n],
            device_id={"batch": partner},
            device_id_type=MESH,
        )

    def span(start, size):
        return pl.ds(pl.multiple_of(start, 16), size)

    def transfer(stage, step, side):
        u, base = UNITS[stage], BASES[stage]
        start = base + 4 * u * side
        half_rows = BASES[stage] // 2 + 2 * u * side
        quarter_rows = BASES[stage] // 4 + u * side
        one, two = keeps[side], keeps[1 - side]
        near, far = partners[side], partners[1 - side]
        if step == 0:
            return across(
                own.at[span(start + 2 * u * (1 - one), 2 * u)],
                first_got.at[span(half_rows, 2 * u)],
                stage,
                step,
                side,
                near,
            )
        if step == 1:
            return across(
                second.at[span(half_rows + u * (1 - two), u)],
                second_got.at[span(quarter_rows, u)],
                stage,
                step,
                side,
                far,
            )
        if step == 2:
            rows = span(start + 2 * u * one + u * two, u)
            return across(whole.at[rows], whole.at[rows], stage, step, side, far)
        rows = span(start + 2 * u * one, 2 * u)
        return across(whole.at[rows], whole.at[rows], stage, step, side, near)

    def advance(stage, step):
        u, base = UNITS[stage], BASES[stage]
        for side in range(2):
            start = base + 4 * u * side
            half_rows = BASES[stage] // 2 + 2 * u * side
            quarter_rows = BASES[stage] // 4 + u * side
            one, two = keeps[side], keeps[1 - side]
            if step > 0:
                transfer(stage, step - 1, side).wait()
            if step == 1:
                mine = own[span(start + 2 * u * one, 2 * u), :].astype(F32)
                theirs = first_got[span(half_rows, 2 * u), :].astype(F32)
                second[span(half_rows, 2 * u), :] = (mine + theirs).astype(BF16)
            if step == 2:
                mine = second[span(half_rows + u * two, u), :].astype(F32)
                theirs = second_got[span(quarter_rows, u), :].astype(F32)
                whole[span(start + 2 * u * one + u * two, u), :] = (mine + theirs).astype(BF16)
            if step < 4:
                transfer(stage, step, side).start()

    def slot(t):
        for stage in range(4):
            if 0 <= t - stage <= 4:
                advance(stage, t - stage)

    own[0:VM, :] = acc_one[...].astype(BF16)
    own[VM : VM + HID, :] = acc_two[...].astype(BF16)
    own[VM + HID : VM + HID + FEAT, :] = acc_out[:FEAT, :].astype(BF16)
    column = iota((COMP, 128), 1)
    diagonal = jnp.where(column < G, acc_lines[:COMP, :], 0.0)
    diagonal = jnp.where((column >= G) & (column < 2 * G), acc_lines[COMP : 2 * COMP, :], diagonal)
    diagonal = jnp.where(
        (column >= 2 * G) & (column < 3 * G), acc_lines[2 * COMP :, :], diagonal
    )
    own[VM + HID + FEAT : BASES[1], :] = diagonal.astype(BF16)
    slot(0)

    dec.others(dec.receive)
    total = dec_got[0]
    for j in range(1, BRICKS):
        total = total + dec_got[j]
    small_sent[0:8] = total
    small_sent[8:16] = jnp.concatenate(
        [acc_bias[0:1, :], acc_out[FEAT : FEAT + 1, :], jnp.zeros((6, 128), F32)], axis=0
    )

    def small_copy(d, peer):
        return pltpu.make_async_remote_copy(
            src_ref=small_sent,
            dst_ref=small_got.at[x],
            send_sem=small_ss.at[d],
            recv_sem=small_rs.at[d],
            device_id={"batch": peer},
            device_id_type=MESH,
        )

    for d, peer in enumerate(x_peers):
        small_copy(d, peer).start()
    small_got[x] = small_sent[...]

    def spread_copy(peer, slot):
        return pltpu.make_async_remote_copy(
            src_ref=dec_all.at[me],
            dst_ref=dec_all.at[slot],
            send_sem=all_ss.at[peer],
            recv_sem=all_rs.at[slot],
            device_id={"brick": peer},
            device_id_type=MESH,
        )

    for pair in range(3):
        a, b, line = PAIRS[pair]
        acc_planes[...] = jnp.zeros_like(acc_planes)

        def scatter(q, carry):
            peers = [at.peer(q, j) for j in range(PEERS)]
            lanes = pl.ds(pl.multiple_of(q * CHUNK, CHUNK), CHUNK)
            points = iota((G, CHUNK), 0, F32)
            other_hat = hat(coordinate(pos_got, peers, b) - points)
            stripe, weights = stripe_weights(coordinate(pos_got, peers, a), other_hat)
            piece = line_s[COMP * pair : COMP * pair + COMP, lanes]
            masked = [
                piece * jnp.where(stripe == float(h), 1.0, 0.0).astype(BF16)
                for h in range(STRIPES)
            ]
            acc_planes[...] += nt(jnp.concatenate(masked, axis=0), weights)
            return carry

        lax.fori_loop(0, CHUNKS, scatter, 0)
        side = STRIPE * G
        acc_planes[COMP:, :G] += acc_planes[: WIDE - COMP, side:]
        turned = nt(eye(side), acc_planes[:, :side].astype(BF16)).astype(BF16)
        base = BASES[pair + 1]
        for tile in range(3):
            own[base + side * tile : base + side * tile + side, :] = turned[
                :, 128 * tile : 128 * tile + 128
            ]
        own[base + 3 * side : base + 640, :] = jnp.zeros((640 - 3 * side, 128), BF16)
        slot(pair + 1)
        if pair == 0:
            for d, peer in enumerate(x_peers):
                small_copy(d, peer).wait()
            small = (small_got[0] + small_got[1]) + (small_got[2] + small_got[3])
            small_sums[...] = small
            dec_all[me] = small[0:8]
            dec.others(lambda peer: spread_copy(peer, me).start())
    for t in range(4, 8):
        slot(t)
    dec.others(lambda peer: spread_copy(peer, peer).wait_recv())
    dec.others(lambda peer: spread_copy(peer, me).wait_send())
    for exchange in (pos, msg, back, dec):
        exchange.sends_done()
    decoder_sums[...] = dec_all[...]
    whole_out[...] = whole[...]


def unpack(
    whole,
    decoder_sums,
    small_sums,
    planes,
    lines,
    one,
    two,
    out,
    head,
    bias,
    decoder_in,
    decoder_out,
    objective,
):
    side = STRIPE * G
    unit = eye(WIDE)
    for pair in range(3):
        base = BASES[pair + 1]
        parts = [whole[base + side * t : base + side * t + side, :] for t in range(3)]
        turned = nt(unit, jnp.concatenate(parts, axis=1))
        for h in range(STRIPES):
            planes[0, COMP * pair : COMP * pair + COMP, side * h : side * h + side] = turned[
                COMP * h : COMP * h + COMP
            ]
    one[0] = whole[0:VM, :].astype(F32)
    two[0] = whole[VM : VM + HID, :].astype(F32)
    out[0] = whole[VM + HID : VM + HID + FEAT, :].astype(F32)
    block = whole[VM + HID + FEAT : BASES[1], :]
    row, column = iota((G, 128), 0), iota((G, 128), 1)
    parts = []
    for p in range(3):
        pick = jnp.where(column == row + G * p, 1.0, 0.0).astype(BF16)
        parts.append(nt(pick, block))
    lines[0] = jnp.concatenate(parts, axis=1)
    bias[...] = small_sums[8:9, 0:1]
    head[...] = small_sums[9:10, :]
    for j in range(8):
        decoder_in[8 * j : 8 * j + 8, 0:128] = decoder_sums[j]
        decoder_in[8 * j : 8 * j + 8, 128:256] = decoder_sums[8 + j]
    last = decoder_sums[16]
    decoder_out[:, 0:128] = last[0:3]
    decoder_out[:, 128:256] = last[3:6]
    objective[...] = last[6:7, 0:1]


def shape(dims, kind=F32):
    return jax.ShapeDtypeStruct(dims, kind)


def on_device(
    crossings,
    lattice,
    offsets,
    target,
    planes,
    line_factors,
    layer_one,
    layer_two,
    layer_out,
    density_head,
    density_bias,
    decoder_in,
    decoder_out,
):
    dma = pltpu.SemaphoreType.DMA
    vmem = pltpu.VMEM
    whole, decoder_sums, small_sums = pl.pallas_call(
        train,
        out_shape=(shape((PACK, 128), BF16), shape((BRICKS, 8, 128)), shape((16, 128))),
        in_specs=[VMEM_SPEC] * 10 + [SMEM_SPEC] + [VMEM_SPEC] * 2,
        out_specs=[VMEM_SPEC] * 3,
        scratch_shapes=[vmem((BRICKS, 8, 128), F32)] * 2
        + [vmem((BRICKS, MSG, 128), BF16)] * 4
        + [vmem((BRICKS, 8, 128), F32)] * 3
        + [vmem((16, 128), F32), vmem((BATCH, 16, 128), F32)]
        + [vmem((RAYS, SLOTS), BF16), vmem((8, SLOTS), F32)]
        + [
            vmem((3, WIDE, LOCAL), BF16),
            vmem((VM, 128), BF16),
            vmem((HID, VM), BF16),
            vmem((HID, HID), BF16),
            vmem((AUG, HID), BF16),
            vmem((HID, AUG), BF16),
        ]
        + [vmem((VM, SAMPLES), BF16)] * 3
        + [vmem((HID, SAMPLES), BF16)] * 4
        + [vmem((FEAT, SAMPLES), BF16), vmem((8, SAMPLES), F32)]
        + [
            vmem((FEAT, SLOTS), F32),
            vmem((WIDE, LOCAL), F32),
            vmem((VM, 128), F32),
            vmem((VM, HID), F32),
            vmem((HID, HID), F32),
            vmem((AUG, HID), F32),
            vmem((8, 128), F32),
        ]
        + [
            vmem((PACK, 128), BF16),
            vmem((PACK // 2, 128), BF16),
            vmem((PACK // 2, 128), BF16),
            vmem((PACK // 4, 128), BF16),
            vmem((PACK, 128), BF16),
        ]
        + [dma((BRICKS,))] * 10
        + [dma((BATCH - 1,))] * 2
        + [dma((32,))] * 2,
        compiler_params=pltpu.CompilerParams(collective_id=0, has_side_effects=True),
        name="train",
    )(
        crossings.T,
        lattice,
        offsets,
        target,
        jnp.swapaxes(planes, 1, 2),
        line_factors,
        layer_one,
        layer_two,
        jnp.swapaxes(layer_out, 1, 2),
        density_head,
        density_bias,
        decoder_in,
        decoder_out,
    )
    outs = pl.pallas_call(
        unpack,
        out_shape=(
            shape((1, VM, G * G)),
            shape((1, G, VM)),
            shape((1, VM, HID)),
            shape((1, HID, HID)),
            shape((1, FEAT, HID)),
            shape((1, HID)),
            shape((1, 1)),
            shape((FEAT, DEC)),
            shape((3, DEC)),
            shape((1, 1)),
        ),
        in_specs=[VMEM_SPEC] * 3,
        out_specs=[VMEM_SPEC] * 10,
        name="unpack",
    )(whole, decoder_sums, small_sums)
    outs = list(outs)
    outs[0] = jnp.swapaxes(outs[0], 1, 2)
    outs[4] = jnp.swapaxes(outs[4], 1, 2)
    outs[6] = outs[6].reshape(1)
    outs[9] = outs[9].reshape(())
    return tuple(outs)

def solution(mesh):
    placed = (
        P(("brick", "batch"), None),
        P(None, None, None, ("brick", "batch")),
        P(None, None, None, ("brick", "batch")),
        P(None, ("brick", "batch")),
        P("brick", None, None),
        P("brick", None, None),
        P("brick", None, None),
        P("brick", None, None),
        P("brick", None, None),
        P("brick", None),
        P("brick"),
        P(),
        P(),
    )
    return jax.shard_map(
        on_device,
        mesh=mesh,
        in_specs=placed,
        out_specs=(
            P("brick", None, None),
            P("brick", None, None),
            P("brick", None, None),
            P("brick", None, None),
            P("brick", None, None),
            P("brick", None),
            P("brick"),
            P(),
            P(),
            P(),
        ),
        check_vma=False,
    )
```

profile of v0, /device:TPU:0, one launch (start us, length us, event | category | flops | bytes accessed | tf_op | source)
XLA Modules:
  0.0 83.9 jit_solution(5745964539153247047)
XLA Ops:
  1.3 79.8 %train.1 = (bf16[2304,128]{1,0:T(8,128)(2,1)}, f32[32,8,128]{2,1,0:T(8,128)}, f32[16,128]{1,0:T(8,128)}) custom-call(s32[8,128]{1,0:T(8,128)} %bitcast.9, s32[3,8,4,128]{3,2,1,0:T(4,128)} %lattice.1, f32[3,8,4,128]{3,2,1,0:T(4,128)} %offsets.1, f32[3,128]{1,0:T(4,128)} %target.1, bf16[1,144,1600]{2,1,0:T(8,128)(2,1)} %bitcast.7, ...), custom_call_target="tpu_custom_call" | custom-call | tf_op jit(solution)/shard_map/train/pallas_call | solution.py:842
  81.1 2.8 %unpack.1 = (f32[1,144,1600]{2,1,0:T(8,128)}, f32[1,40,144]{2,1,0:T(8,128)}, f32[1,144,128]{2,1,0:T(8,128)}, f32[1,128,128]{2,1,0:T(8,128)}, f32[1,64,128]{2,1,0...) custom-call(bf16[2304,128]{1,0:T(8,128)(2,1)} %get-tuple-element.23., ...), custom_call_target="tpu_custom_call" | custom-call | tf_op jit(solution)/shard_map/unpack/pallas_call | solution.py:899
where the time goes:
time: 84.5 us; the launch traced here: 83.9 us
  Pallas kernels  82.6 us (98%)
  between operations  1.3 us (2%)
    pallas_call x1, Pallas kernels, on_device(): pl.pallas_call(train, out_shape=(shape((PACK, 128), BF16), shape((BRICKS,...  79.8 us
    pallas_call x1, Pallas kernels, on_device(): pl.pallas_call(unpack, out_shape=(shape((1, VM, G * G)), shape((1, G, VM)...  2.77 us

commit v1 on v0

--- a/solution.py
+++ b/solution.py
@@ -30,6 +30,7 @@
 PEERS = 4
 CHUNK = PEERS * 256
 CHUNKS = BRICKS // PEERS
+GROUP = 4
 SAMPLES = BRICKS * CAP * 4
 MSG = 40
 HALF = FEAT // 2
@@ -146,6 +147,7 @@
     two_t,
     out_t,
     out_aug,
+    two_half,
 ):
     for h in range(STRIPES):
         at = STRIPE * G * h
@@ -165,8 +167,9 @@
     )
     line_t[...] = jnp.where(keep, wide, 0.0).astype(BF16)
     unit = eye(HID)
-    one_t[...] = nt(unit, layer_one[0]).astype(BF16)
-    two_t[...] = nt(unit, layer_two[0]).astype(BF16)
+    one_t[...] = (0.5 * nt(unit, layer_one[0])).astype(BF16)
+    two_t[...] = (0.5 * nt(unit, layer_two[0])).astype(BF16)
+    two_half[...] = (0.5 * layer_two[0].astype(F32)).astype(BF16)
     rows = [
         layer_out[0].astype(F32),
         density_head[...].astype(F32),
@@ -174,7 +177,7 @@
     ]
     both = jnp.concatenate(rows, axis=0).astype(BF16)
     out_t[...] = both
-    out_aug[...] = nt(unit, both).astype(BF16)
+    out_aug[...] = (0.5 * nt(unit, both)).astype(BF16)
 
 
 def coordinate(positions, peers, c):
@@ -187,7 +190,7 @@
 def stripe_weights(along, other_hat):
     stripe = jnp.floor(along * (1.0 / STRIPE))
     local = along - float(STRIPE) * stripe
-    near = hat(local - iota((8, CHUNK), 0, F32))
+    near = hat(local - iota((8, along.shape[1]), 0, F32))
     weights = jnp.concatenate(
         [near[i : i + 1] * other_hat for i in range(STRIPE + 1)], axis=0
     ).astype(BF16)
@@ -195,7 +198,7 @@
 
 
 def line_table(hats):
-    rows = [hats[PAIRS[p][2]] for p in range(3)] + [jnp.zeros((8, CHUNK), F32)]
+    rows = [hats[PAIRS[p][2]] for p in range(3)] + [jnp.zeros((8, hats[0].shape[1]), F32)]
     return jnp.concatenate(rows, axis=0).astype(BF16)
 
 
@@ -225,6 +228,22 @@
     out = mm(jnp.concatenate(split3(table), axis=0), ray_slots)
     out = out[0:8] + out[8:16] + out[16:24]
     return jnp.sum(out * cross_mask, axis=0, keepdims=True)
+
+
+def silu_of_half(u, hidden, slope, lanes):
+    t = jnp.tanh(u)
+    p = 1.0 + t
+    v = u * p
+    h = v.astype(BF16)
+    hidden[:, lanes] = h
+    slope[:, lanes] = (p + v * (1.0 - t)).astype(BF16)
+    return h
+
+
+def together(*parts):
+    parts = list(parts)
+    while parts:
+        parts = [part for part in parts if next(part, parts) is not parts]
 
 
 class Brick:
@@ -310,6 +329,7 @@
     two_t,
     out_t,
     out_aug,
+    two_half,
     vm_s,
     plane_s,
     line_s,
@@ -397,11 +417,12 @@
         two_t,
         out_t,
         out_aug,
+        two_half,
     )
     for ref in (acc_lines, acc_one, acc_two, acc_out, acc_bias, dec_sent):
         ref[...] = jnp.zeros_like(ref)
 
-    def forward(q, carry):
+    def look_up(q):
         peers = [at.peer(q, j) for j in range(PEERS)]
         for p in peers:
 
@@ -413,38 +434,38 @@
         coords = [coordinate(pos_got, peers, c) for c in range(3)]
         points = iota((G, CHUNK), 0, F32)
         hats = [hat(coord - points) for coord in coords]
-        values = []
+        line_value = mm(line_t[...], line_table(hats))
+        line_s[:, lanes] = line_value.astype(BF16)
         for pair in range(3):
             a, b, line = PAIRS[pair]
             stripe, weights = stripe_weights(coords[a], hats[b])
             wide = mm(plane_t[pair], weights)
-            value = wide[:COMP]
-            for h in range(1, STRIPES):
-                value = jnp.where(stripe == float(h), wide[COMP * h : COMP * h + COMP], value)
-            values.append(value)
-        plane_value = jnp.concatenate(values, axis=0)
-        line_value = mm(line_t[...], line_table(hats))
-        vm = (plane_value * line_value).astype(BF16)
-        vm_s[:, lanes] = vm
-        plane_s[:, lanes] = plane_value.astype(BF16)
-        line_s[:, lanes] = line_value.astype(BF16)
-        a1 = mm(one_t[...], vm)
-        g1 = sigmoid(a1)
-        v1 = a1 * g1
-        h1 = v1.astype(BF16)
-        h1_s[:, lanes] = h1
-        s1_s[:, lanes] = (g1 + v1 * (1.0 - g1)).astype(BF16)
-        a2 = mm(two_t[...], h1)
-        g2 = sigmoid(a2)
-        v2 = a2 * g2
-        h2 = v2.astype(BF16)
-        h2_s[:, lanes] = h2
-        s2_s[:, lanes] = (g2 + v2 * (1.0 - g2)).astype(BF16)
+            stripe = jnp.broadcast_to(stripe, (8, CHUNK))
+            masks = [stripe == float(h) for h in range(STRIPES)]
+            values = []
+            for r in range(0, COMP, 8):
+                value = wide[r : r + 8]
+                for h in range(1, STRIPES):
+                    value = jnp.where(masks[h], wide[COMP * h + r : COMP * h + r + 8], value)
+                values.append(value)
+            value = jnp.concatenate(values, axis=0)
+            rows = slice(COMP * pair, COMP * pair + COMP)
+            vm_s[rows, lanes] = (value * line_value[rows]).astype(BF16)
+            plane_s[rows, lanes] = value.astype(BF16)
+            yield
+
+    def network(q):
+        peers = [at.peer(q, j) for j in range(PEERS)]
+        lanes = pl.ds(pl.multiple_of(q * CHUNK, CHUNK), CHUNK)
+        h1 = silu_of_half(mm(one_t[...], vm_s[:, lanes]), h1_s, s1_s, lanes)
+        yield
+        h2 = silu_of_half(mm(two_t[...], h1), h2_s, s2_s, lanes)
         wide = mm(out_t[...], h2)
         feat = wide[:FEAT].astype(BF16)
         feat_s[:, lanes] = feat
         zeta = wide[FEAT : FEAT + 1] + bias[0]
         zeta_s[:, lanes] = jnp.broadcast_to(zeta, (8, CHUNK))
+        yield
         low = low_half((HALF, 128))
         for j, p in enumerate(peers):
             depths, befores, total = within_crossing(zeta, j)
@@ -458,14 +479,20 @@
             parts = [part.astype(F32) for part in split3(total)]
             rows = [folded] + parts + [jnp.zeros((MSG - HALF - 3, 128), F32)]
             msg_sent[p] = jnp.concatenate(rows, axis=0).astype(BF16)
+        yield
+        for p in peers:
 
             @pl.when(p != me)
             def _():
                 msg.send(p)
 
+    def forward(q, carry):
+        together(look_up(q + 1), network(q))
         return carry
 
-    lax.fori_loop(0, CHUNKS, forward, 0)
+    together(look_up(0))
+    lax.fori_loop(0, CHUNKS - 1, forward, 0)
+    together(network(CHUNKS - 1))
     msg_got[me] = msg_sent[me]
 
     ray_slots = ray_slots_ref[...]
@@ -592,7 +619,7 @@
         acc_out[...] += nt(grad_aug, h2_s[:, lanes])
         grad_a2 = (mm(out_aug[...], grad_aug) * s2_s[:, lanes].astype(F32)).astype(BF16)
         acc_two[...] += nt(h1_s[:, lanes], grad_a2)
-        grad_a1 = (mm(layer_two[0], grad_a2) * s1_s[:, lanes].astype(F32)).astype(BF16)
+        grad_a1 = (mm(two_half[...], grad_a2) * s1_s[:, lanes].astype(F32)).astype(BF16)
         acc_one[...] += nt(vm_s[:, lanes], grad_a1)
         grad_vm = mm(layer_one[0], grad_a1)
         grad_line = (grad_vm * plane_s[:, lanes].astype(F32)).astype(BF16)
@@ -730,21 +757,28 @@
         a, b, line = PAIRS[pair]
         acc_planes[...] = jnp.zeros_like(acc_planes)
 
-        def scatter(q, carry):
-            peers = [at.peer(q, j) for j in range(PEERS)]
-            lanes = pl.ds(pl.multiple_of(q * CHUNK, CHUNK), CHUNK)
-            points = iota((G, CHUNK), 0, F32)
-            other_hat = hat(coordinate(pos_got, peers, b) - points)
-            stripe, weights = stripe_weights(coordinate(pos_got, peers, a), other_hat)
-            piece = line_s[COMP * pair : COMP * pair + COMP, lanes]
-            masked = [
-                piece * jnp.where(stripe == float(h), 1.0, 0.0).astype(BF16)
-                for h in range(STRIPES)
-            ]
-            acc_planes[...] += nt(jnp.concatenate(masked, axis=0), weights)
+        def scatter(g, carry):
+            masked, weights = [], []
+            for q in range(GROUP):
+                q = g * GROUP + q
+                peers = [at.peer(q, j) for j in range(PEERS)]
+                lanes = pl.ds(pl.multiple_of(q * CHUNK, CHUNK), CHUNK)
+                points = iota((G, CHUNK), 0, F32)
+                other_hat = hat(coordinate(pos_got, peers, b) - points)
+                stripe, weight = stripe_weights(coordinate(pos_got, peers, a), other_hat)
+                piece = line_s[COMP * pair : COMP * pair + COMP, lanes]
+                rows = [
+                    piece * jnp.where(stripe == float(h), 1.0, 0.0).astype(BF16)
+                    for h in range(STRIPES)
+                ]
+                masked.append(jnp.concatenate(rows, axis=0))
+                weights.append(weight)
+            acc_planes[...] += nt(
+                jnp.concatenate(masked, axis=1), jnp.concatenate(weights, axis=1)
+            )
             return carry
 
-        lax.fori_loop(0, CHUNKS, scatter, 0)
+        lax.fori_loop(0, CHUNKS // GROUP, scatter, 0)
         side = STRIPE * G
         acc_planes[COMP:, :G] += acc_planes[: WIDE - COMP, side:]
         turned = nt(eye(side), acc_planes[:, :side].astype(BF16)).astype(BF16)
@@ -856,6 +890,7 @@
             vmem((HID, HID), BF16),
             vmem((AUG, HID), BF16),
             vmem((HID, AUG), BF16),
+            vmem((HID, HID), BF16),
         ]
         + [vmem((VM, SAMPLES), BF16)] * 3
         + [vmem((HID, SAMPLES), BF16)] * 4

time: 84.5 us -> 80.2 us (0.949)
  Pallas kernels: 82.6 us -> 78.2 us
    pallas_call x1, Pallas kernels: 79.8 us -> 75.4 us  [on_device(): pl.pallas_call(train, out_shape=(shape((PACK, 128), BF16), shape((BRICKS,...]
where the time goes in v1:
time: 80.2 us; the launch traced here: 79.5 us
  Pallas kernels  78.2 us (98%)
  between operations  1.3 us (2%)
    pallas_call x1, Pallas kernels, on_device(): pl.pallas_call(train, out_shape=(shape((PACK, 128), BF16), shape((BRICKS,...  75.4 us
    pallas_call x1, Pallas kernels, on_device(): pl.pallas_call(unpack, out_shape=(shape((1, VM, G * G)), shape((1, G, VM)...  2.77 us

profile of v1, /device:TPU:0, one launch (start us, length us, event | category | flops | bytes accessed | tf_op | source)
XLA Modules:
  0.0 79.5 jit_solution(8059394303428247138)
XLA Ops:
  1.3 75.4 %train.1 = (bf16[2304,128]{1,0:T(8,128)(2,1)}, f32[32,8,128]{2,1,0:T(8,128)}, f32[16,128]{1,0:T(8,128)}) custom-call(s32[8,128]{1,0:T(8,128)} %bitcast.9, s32[3,8,4,128]{3,2,1,0:T(4,128)} %lattice.1, f32[3,8,4,128]{3,2,1,0:T(4,128)} %offsets.1, f32[3,128]{1,0:T(4,128)} %target.1, bf16[1,144,1600]{2,1,0:T(8,128)(2,1)} %bitcast.7, ...), custom_call_target="tpu_custom_call" | custom-call | tf_op jit(solution)/shard_map/train/pallas_call | solution.py:876
  76.7 2.8 %unpack.1 = (f32[1,144,1600]{2,1,0:T(8,128)}, f32[1,40,144]{2,1,0:T(8,128)}, f32[1,144,128]{2,1,0:T(8,128)}, f32[1,128,128]{2,1,0:T(8,128)}, f32[1,64,128]{2,1,0...) custom-call(bf16[2304,128]{1,0:T(8,128)(2,1)} %get-tuple-element.23., ...), custom_call_target="tpu_custom_call" | custom-call | tf_op jit(solution)/shard_map/unpack/pallas_call | solution.py:934

commit v2 on v1

--- a/solution.py
+++ b/solution.py
@@ -34,8 +34,8 @@
 SAMPLES = BRICKS * CAP * 4
 MSG = 40
 HALF = FEAT // 2
-UNITS = (48, 80, 80, 80)
-BASES = (0, 384, 1024, 1664)
+UNITS = (80, 80, 80, 48)
+BASES = (0, 640, 1280, 1920)
 PACK = 2304
 PAIRS = ((0, 1, 2), (0, 2, 1), (1, 2, 0))
 VMEM_SPEC = pl.BlockSpec(memory_space=pltpu.VMEM)
@@ -307,7 +307,8 @@
     bias,
     decoder_in,
     decoder_out,
-    whole_out,
+    planes_out,
+    layers_out,
     decoder_sums,
     small_sums,
     pos_sent,
@@ -321,6 +322,9 @@
     dec_all,
     small_sent,
     small_got,
+    head_sent,
+    head_got,
+    aug_s,
     ray_slots_ref,
     slot_cross,
     plane_t,
@@ -351,6 +355,8 @@
     second,
     second_got,
     whole,
+    pair_got,
+    pair_sum,
     pos_ss,
     pos_rs,
     msg_ss,
@@ -363,6 +369,8 @@
     all_rs,
     small_ss,
     small_rs,
+    head_ss,
+    head_rs,
     sum_ss,
     sum_rs,
 ):
@@ -566,8 +574,6 @@
         dec_sent[8 + j] = grad_in[8 * j : 8 * j + 8, 128:]
     rows = [grad_out[:, :128], grad_out[:, 128:], jnp.full((2, 128), objective, F32)]
     dec_sent[16] = jnp.concatenate(rows, axis=0)
-    dec.others(dec.send)
-    dec_got[me] = dec_sent[me]
 
     def backward(i, carry):
         q = CHUNKS - 1 - i
@@ -616,20 +622,19 @@
         rows = [jnp.concatenate(grad_feats, axis=1), grad_zeta]
         rows.append(jnp.zeros((AUG - FEAT - 1, CHUNK), F32))
         grad_aug = jnp.concatenate(rows, axis=0).astype(BF16)
-        acc_out[...] += nt(grad_aug, h2_s[:, lanes])
+        aug_s[:, lanes] = grad_aug
         grad_a2 = (mm(out_aug[...], grad_aug) * s2_s[:, lanes].astype(F32)).astype(BF16)
-        acc_two[...] += nt(h1_s[:, lanes], grad_a2)
+        s2_s[:, lanes] = grad_a2
         grad_a1 = (mm(two_half[...], grad_a2) * s1_s[:, lanes].astype(F32)).astype(BF16)
-        acc_one[...] += nt(vm_s[:, lanes], grad_a1)
+        s1_s[:, lanes] = grad_a1
         grad_vm = mm(layer_one[0], grad_a1)
-        grad_line = (grad_vm * plane_s[:, lanes].astype(F32)).astype(BF16)
+        plane_s[:, lanes] = (grad_vm * plane_s[:, lanes].astype(F32)).astype(BF16)
         line_s[:, lanes] = (grad_vm * line_s[:, lanes].astype(F32)).astype(BF16)
-        points = iota((G, CHUNK), 0, F32)
-        hats = [hat(coordinate(pos_got, peers, c) - points) for c in range(3)]
-        acc_lines[...] += nt(grad_line, line_table(hats))
         return carry
 
     lax.fori_loop(0, CHUNKS, backward, 0)
+    dec.others(dec.send)
+    dec_got[me] = dec_sent[me]
 
     partner_a = x + 1 - 2 * lax.rem(x, 2)
     partner_b = BATCH - 1 - x
@@ -703,31 +708,50 @@
             if step < 4:
                 transfer(stage, step, side).start()
 
+    def exchange_half(stage, step, side):
+        u = UNITS[stage]
+        start = BASES[stage] + 4 * u * side
+        at_row = start - BASES[2]
+        rows = pl.ds(at_row, 4 * u)
+        if step == 0:
+            src, partner = own.at[pl.ds(start, 4 * u)], partners[side]
+        else:
+            src, partner = pair_sum.at[rows], partners[1 - side]
+        return across(src, pair_got.at[step].at[rows], stage, step, side, partner)
+
+    def advance_doubling(stage, step):
+        u = UNITS[stage]
+        for side in range(2):
+            start = BASES[stage] + 4 * u * side
+            at_row = start - BASES[2]
+            if step > 0:
+                exchange_half(stage, step - 1, side).wait()
+                theirs = pair_got[step - 1, at_row : at_row + 4 * u, :].astype(F32)
+            if step == 1:
+                mine = own[start : start + 4 * u, :].astype(F32)
+                pair_sum[at_row : at_row + 4 * u, :] = (mine + theirs).astype(BF16)
+            if step == 2:
+                mine = pair_sum[at_row : at_row + 4 * u, :].astype(F32)
+                whole[start : start + 4 * u, :] = (mine + theirs).astype(BF16)
+            if step < 2:
+                exchange_half(stage, step, side).start()
+
     def slot(t):
-        for stage in range(4):
-            if 0 <= t - stage <= 4:
-                advance(stage, t - stage)
-
-    own[0:VM, :] = acc_one[...].astype(BF16)
-    own[VM : VM + HID, :] = acc_two[...].astype(BF16)
-    own[VM + HID : VM + HID + FEAT, :] = acc_out[:FEAT, :].astype(BF16)
-    column = iota((COMP, 128), 1)
-    diagonal = jnp.where(column < G, acc_lines[:COMP, :], 0.0)
-    diagonal = jnp.where((column >= G) & (column < 2 * G), acc_lines[COMP : 2 * COMP, :], diagonal)
-    diagonal = jnp.where(
-        (column >= 2 * G) & (column < 3 * G), acc_lines[2 * COMP :, :], diagonal
-    )
-    own[VM + HID + FEAT : BASES[1], :] = diagonal.astype(BF16)
-    slot(0)
-
-    dec.others(dec.receive)
-    total = dec_got[0]
-    for j in range(1, BRICKS):
-        total = total + dec_got[j]
-    small_sent[0:8] = total
-    small_sent[8:16] = jnp.concatenate(
-        [acc_bias[0:1, :], acc_out[FEAT : FEAT + 1, :], jnp.zeros((6, 128), F32)], axis=0
-    )
+        for stage in reversed(range(4)) if t > 3 else range(4):
+            step = t - stage
+            if stage < 2 and 0 <= step <= 4:
+                advance(stage, step)
+            if stage >= 2 and 0 <= step <= 2:
+                advance_doubling(stage, step)
+
+    def settle(pair):
+        side, base = STRIPE * G, BASES[pair]
+        parts = [whole[base + side * t : base + side * t + side, :] for t in range(3)]
+        turned = nt(eye(WIDE), jnp.concatenate(parts, axis=1)).astype(BF16)
+        for h in range(STRIPES):
+            planes_out[COMP * pair : COMP * pair + COMP, side * h : side * h + side] = turned[
+                COMP * h : COMP * h + COMP
+            ]
 
     def small_copy(d, peer):
         return pltpu.make_async_remote_copy(
@@ -738,10 +762,6 @@
             device_id={"batch": peer},
             device_id_type=MESH,
         )
-
-    for d, peer in enumerate(x_peers):
-        small_copy(d, peer).start()
-    small_got[x] = small_sent[...]
 
     def spread_copy(peer, slot):
         return pltpu.make_async_remote_copy(
@@ -782,32 +802,96 @@
         side = STRIPE * G
         acc_planes[COMP:, :G] += acc_planes[: WIDE - COMP, side:]
         turned = nt(eye(side), acc_planes[:, :side].astype(BF16)).astype(BF16)
-        base = BASES[pair + 1]
+        base = BASES[pair]
         for tile in range(3):
             own[base + side * tile : base + side * tile + side, :] = turned[
                 :, 128 * tile : 128 * tile + 128
             ]
         own[base + 3 * side : base + 640, :] = jnp.zeros((640 - 3 * side, 128), BF16)
-        slot(pair + 1)
+        slot(pair)
         if pair == 0:
+            dec.others(dec.receive)
+            total = dec_got[0]
+            for j in range(1, BRICKS):
+                total = total + dec_got[j]
+            small_sent[0:8] = total
+            small_sent[8:16] = jnp.concatenate(
+                [acc_bias[0:1, :], jnp.zeros((7, 128), F32)], axis=0
+            )
+            for d, peer in enumerate(x_peers):
+                small_copy(d, peer).start()
+            small_got[x] = small_sent[...]
+        if pair == 1:
             for d, peer in enumerate(x_peers):
                 small_copy(d, peer).wait()
             small = (small_got[0] + small_got[1]) + (small_got[2] + small_got[3])
-            small_sums[...] = small
+            small_sums[0:8] = small[8:16]
             dec_all[me] = small[0:8]
             dec.others(lambda peer: spread_copy(peer, me).start())
-    for t in range(4, 8):
-        slot(t)
+    def layers(g, carry):
+        tables = []
+        for q in range(GROUP):
+            q = g * GROUP + q
+            peers = [at.peer(q, j) for j in range(PEERS)]
+            points = iota((G, CHUNK), 0, F32)
+            hats = [hat(coordinate(pos_got, peers, c) - points) for c in range(3)]
+            tables.append(line_table(hats))
+        lanes = pl.ds(pl.multiple_of(g * GROUP * CHUNK, GROUP * CHUNK), GROUP * CHUNK)
+        acc_lines[...] += nt(plane_s[:, lanes], jnp.concatenate(tables, axis=1))
+        acc_out[...] += nt(aug_s[:, lanes], h2_s[:, lanes])
+        acc_two[...] += nt(h1_s[:, lanes], s2_s[:, lanes])
+        acc_one[...] += nt(vm_s[:, lanes], s1_s[:, lanes])
+        return carry
+
+    lax.fori_loop(0, CHUNKS // GROUP, layers, 0)
+    base = BASES[3]
+    own[base : base + VM, :] = acc_one[...].astype(BF16)
+    own[base + VM : base + VM + HID, :] = acc_two[...].astype(BF16)
+    own[base + VM + HID : base + VM + HID + FEAT, :] = acc_out[:FEAT, :].astype(BF16)
+    column = iota((COMP, 128), 1)
+    diagonal = jnp.where(column < G, acc_lines[:COMP, :], 0.0)
+    diagonal = jnp.where((column >= G) & (column < 2 * G), acc_lines[COMP : 2 * COMP, :], diagonal)
+    diagonal = jnp.where(
+        (column >= 2 * G) & (column < 3 * G), acc_lines[2 * COMP :, :], diagonal
+    )
+    own[base + VM + HID + FEAT :, :] = diagonal.astype(BF16)
+    slot(3)
+    head_sent[...] = jnp.broadcast_to(acc_out[FEAT : FEAT + 1, :], (8, 128))
+
+    def head_copy(d, peer):
+        return pltpu.make_async_remote_copy(
+            src_ref=head_sent,
+            dst_ref=head_got.at[x],
+            send_sem=head_ss.at[d],
+            recv_sem=head_rs.at[d],
+            device_id={"batch": peer},
+            device_id_type=MESH,
+        )
+
+    for d, peer in enumerate(x_peers):
+        head_copy(d, peer).start()
+    head_got[x] = head_sent[...]
+    for exchange in (pos, msg):
+        exchange.sends_done()
+    slot(4)
+    settle(0)
+    settle(2)
     dec.others(lambda peer: spread_copy(peer, peer).wait_recv())
+    decoder_sums[...] = dec_all[...]
     dec.others(lambda peer: spread_copy(peer, me).wait_send())
-    for exchange in (pos, msg, back, dec):
+    for exchange in (back, dec):
         exchange.sends_done()
-    decoder_sums[...] = dec_all[...]
-    whole_out[...] = whole[...]
+    for d, peer in enumerate(x_peers):
+        head_copy(d, peer).wait()
+    small_sums[8:16] = (head_got[0] + head_got[1]) + (head_got[2] + head_got[3])
+    slot(5)
+    settle(1)
+    layers_out[...] = whole[BASES[3] :, :]
 
 
 def unpack(
-    whole,
+    planes_in,
+    layers,
     decoder_sums,
     small_sums,
     planes,
@@ -821,28 +905,19 @@
     decoder_out,
     objective,
 ):
-    side = STRIPE * G
-    unit = eye(WIDE)
-    for pair in range(3):
-        base = BASES[pair + 1]
-        parts = [whole[base + side * t : base + side * t + side, :] for t in range(3)]
-        turned = nt(unit, jnp.concatenate(parts, axis=1))
-        for h in range(STRIPES):
-            planes[0, COMP * pair : COMP * pair + COMP, side * h : side * h + side] = turned[
-                COMP * h : COMP * h + COMP
-            ]
-    one[0] = whole[0:VM, :].astype(F32)
-    two[0] = whole[VM : VM + HID, :].astype(F32)
-    out[0] = whole[VM + HID : VM + HID + FEAT, :].astype(F32)
-    block = whole[VM + HID + FEAT : BASES[1], :]
+    planes[0] = planes_in[...].astype(F32)
+    one[0] = layers[0:VM, :].astype(F32)
+    two[0] = layers[VM : VM + HID, :].astype(F32)
+    out[0] = layers[VM + HID : VM + HID + FEAT, :].astype(F32)
+    block = layers[VM + HID + FEAT : PACK - BASES[3], :]
     row, column = iota((G, 128), 0), iota((G, 128), 1)
     parts = []
     for p in range(3):
         pick = jnp.where(column == row + G * p, 1.0, 0.0).astype(BF16)
         parts.append(nt(pick, block))
     lines[0] = jnp.concatenate(parts, axis=1)
-    bias[...] = small_sums[8:9, 0:1]
-    head[...] = small_sums[9:10, :]
+    bias[...] = small_sums[0:1, 0:1]
+    head[...] = small_sums[8:9, :]
     for j in range(8):
         decoder_in[8 * j : 8 * j + 8, 0:128] = decoder_sums[j]
         decoder_in[8 * j : 8 * j + 8, 128:256] = decoder_sums[8 + j]
@@ -873,15 +948,21 @@
 ):
     dma = pltpu.SemaphoreType.DMA
     vmem = pltpu.VMEM
-    whole, decoder_sums, small_sums = pl.pallas_call(
+    planes_sum, layers_sum, decoder_sums, small_sums = pl.pallas_call(
         train,
-        out_shape=(shape((PACK, 128), BF16), shape((BRICKS, 8, 128)), shape((16, 128))),
+        out_shape=(
+            shape((VM, G * G), BF16),
+            shape((PACK - BASES[3], 128), BF16),
+            shape((BRICKS, 8, 128)),
+            shape((16, 128)),
+        ),
         in_specs=[VMEM_SPEC] * 10 + [SMEM_SPEC] + [VMEM_SPEC] * 2,
-        out_specs=[VMEM_SPEC] * 3,
+        out_specs=[VMEM_SPEC] * 4,
         scratch_shapes=[vmem((BRICKS, 8, 128), F32)] * 2
         + [vmem((BRICKS, MSG, 128), BF16)] * 4
         + [vmem((BRICKS, 8, 128), F32)] * 3
         + [vmem((16, 128), F32), vmem((BATCH, 16, 128), F32)]
+        + [vmem((8, 128), F32), vmem((BATCH, 8, 128), F32), vmem((AUG, SAMPLES), BF16)]
         + [vmem((RAYS, SLOTS), BF16), vmem((8, SLOTS), F32)]
         + [
             vmem((3, WIDE, LOCAL), BF16),
@@ -906,13 +987,15 @@
         ]
         + [
             vmem((PACK, 128), BF16),
-            vmem((PACK // 2, 128), BF16),
-            vmem((PACK // 2, 128), BF16),
-            vmem((PACK // 4, 128), BF16),
+            vmem((BASES[2] // 2, 128), BF16),
+            vmem((BASES[2] // 2, 128), BF16),
+            vmem((BASES[2] // 4, 128), BF16),
             vmem((PACK, 128), BF16),
+            vmem((2, PACK - BASES[2], 128), BF16),
+            vmem((PACK - BASES[2], 128), BF16),
         ]
         + [dma((BRICKS,))] * 10
-        + [dma((BATCH - 1,))] * 2
+        + [dma((BATCH - 1,))] * 4
         + [dma((32,))] * 2,
         compiler_params=pltpu.CompilerParams(collective_id=0, has_side_effects=True),
         name="train",
@@ -945,10 +1028,10 @@
             shape((3, DEC)),
             shape((1, 1)),
         ),
-        in_specs=[VMEM_SPEC] * 3,
+        in_specs=[VMEM_SPEC] * 4,
         out_specs=[VMEM_SPEC] * 10,
         name="unpack",
-    )(whole, decoder_sums, small_sums)
+    )(planes_sum, layers_sum, decoder_sums, small_sums)
     outs = list(outs)
     outs[0] = jnp.swapaxes(outs[0], 1, 2)
     outs[4] = jnp.swapaxes(outs[4], 1, 2)

time: 80.2 us -> 76 us (0.948)
  Pallas kernels: 78.2 us -> 74.5 us
    pallas_call x1, Pallas kernels: 75.4 us -> 72.2 us  [on_device(): pl.pallas_call(train, out_shape=(shape((VM, G * G), BF16), shape((PACK -...]
where the time goes in v2:
time: 76 us; the launch traced here: 75.8 us
  Pallas kernels  74.5 us (98%)
  between operations  1.3 us (2%)
    pallas_call x1, Pallas kernels, on_device(): pl.pallas_call(train, out_shape=(shape((VM, G * G), BF16), shape((PACK -...  72.2 us
    pallas_call x1, Pallas kernels, on_device(): pl.pallas_call(unpack, out_shape=(shape((1, VM, G * G)), shape((1, G, VM)...  2.3 us

profile of v2, /device:TPU:0, one launch (start us, length us, event | category | flops | bytes accessed | tf_op | source)
XLA Modules:
  0.0 75.8 jit_solution(15387635505322396190)
XLA Ops:
  1.3 72.2 %train.1 = (bf16[144,1600]{1,0:T(8,128)(2,1)}, bf16[384,128]{1,0:T(8,128)(2,1)}, f32[32,8,128]{2,1,0:T(8,128)}, f32[16,128]{1,0:T(8,128)}) custom-call(s32[8,128]{1,0:T(8,128)} %bitcast.9, s32[3,8,4,128]{3,2,1,0:T(4,128)} %lattice.1, f32[3,8,4,128]{3,2,1,0:T(4,128)} %offsets.1, f32[3,128]{1,0:T(4,128)} %target.1, bf16[1,144,1600]{2,1,0:T(8,128)(2,1)} %bitcast.7, ...), custom_call_target="tpu_custom_call" | custom-call | tf_op jit(solution)/shard_map/train/pallas_call | solution.py:951
  73.5 2.3 %unpack.1 = (f32[1,144,1600]{2,1,0:T(8,128)}, f32[1,40,144]{2,1,0:T(8,128)}, f32[1,144,128]{2,1,0:T(8,128)}, f32[1,128,128]{2,1,0:T(8,128)}, f32[1,64,128]{2,1,0...) custom-call(bf16[144,1600]{1,0:T(8,128)(2,1)} %get-tuple-element.24., ...), custom_call_target="tpu_custom_call" | custom-call | tf_op jit(solution)/shard_map/unpack/pallas_call | solution.py:1017

commit v3 on v2

--- a/solution.py
+++ b/solution.py
@@ -34,9 +34,9 @@
 SAMPLES = BRICKS * CAP * 4
 MSG = 40
 HALF = FEAT // 2
-UNITS = (80, 80, 80, 48)
-BASES = (0, 640, 1280, 1920)
-PACK = 2304
+SIDES = ((0, 304, 600), (600, 904, 1200), (1200, 1504, 1800), (1800, 1992, 2184))
+BASES = (0, 600, 1200, 1800)
+PACK = 2184
 PAIRS = ((0, 1, 2), (0, 2, 1), (1, 2, 0))
 VMEM_SPEC = pl.BlockSpec(memory_space=pltpu.VMEM)
 SMEM_SPEC = pl.BlockSpec(memory_space=pltpu.SMEM)
@@ -351,9 +351,6 @@
     acc_out,
     acc_bias,
     own,
-    first_got,
-    second,
-    second_got,
     whole,
     pair_got,
     pair_sum,
@@ -638,13 +635,10 @@
 
     partner_a = x + 1 - 2 * lax.rem(x, 2)
     partner_b = BATCH - 1 - x
-    keep_a = lax.rem((x + 1) // 2, 2)
-    keep_b = x // 2
     partners = (partner_a, partner_b)
-    keeps = (keep_a, keep_b)
 
     def across(src, dst, stage, step, side, partner):
-        n = (stage * 4 + step) * 2 + side
+        n = (stage * 2 + step) * 2 + side
         return pltpu.make_async_remote_copy(
             src_ref=src,
             dst_ref=dst,
@@ -654,95 +648,23 @@
             device_id_type=MESH,
         )
 
-    def span(start, size):
-        return pl.ds(pl.multiple_of(start, 16), size)
-
-    def transfer(stage, step, side):
-        u, base = UNITS[stage], BASES[stage]
-        start = base + 4 * u * side
-        half_rows = BASES[stage] // 2 + 2 * u * side
-        quarter_rows = BASES[stage] // 4 + u * side
-        one, two = keeps[side], keeps[1 - side]
-        near, far = partners[side], partners[1 - side]
-        if step == 0:
-            return across(
-                own.at[span(start + 2 * u * (1 - one), 2 * u)],
-                first_got.at[span(half_rows, 2 * u)],
-                stage,
-                step,
-                side,
-                near,
-            )
-        if step == 1:
-            return across(
-                second.at[span(half_rows + u * (1 - two), u)],
-                second_got.at[span(quarter_rows, u)],
-                stage,
-                step,
-                side,
-                far,
-            )
-        if step == 2:
-            rows = span(start + 2 * u * one + u * two, u)
-            return across(whole.at[rows], whole.at[rows], stage, step, side, far)
-        rows = span(start + 2 * u * one, 2 * u)
-        return across(whole.at[rows], whole.at[rows], stage, step, side, near)
+    def exchange_half(stage, step, side):
+        start, end = SIDES[stage][side : side + 2]
+        rows = pl.ds(start, end - start)
+        src = (own, pair_sum)[step].at[rows]
+        partner = partners[(side + step) % 2]
+        return across(src, pair_got.at[step].at[rows], stage, step, side, partner)
 
     def advance(stage, step):
-        u, base = UNITS[stage], BASES[stage]
         for side in range(2):
-            start = base + 4 * u * side
-            half_rows = BASES[stage] // 2 + 2 * u * side
-            quarter_rows = BASES[stage] // 4 + u * side
-            one, two = keeps[side], keeps[1 - side]
-            if step > 0:
-                transfer(stage, step - 1, side).wait()
-            if step == 1:
-                mine = own[span(start + 2 * u * one, 2 * u), :].astype(F32)
-                theirs = first_got[span(half_rows, 2 * u), :].astype(F32)
-                second[span(half_rows, 2 * u), :] = (mine + theirs).astype(BF16)
-            if step == 2:
-                mine = second[span(half_rows + u * two, u), :].astype(F32)
-                theirs = second_got[span(quarter_rows, u), :].astype(F32)
-                whole[span(start + 2 * u * one + u * two, u), :] = (mine + theirs).astype(BF16)
-            if step < 4:
-                transfer(stage, step, side).start()
-
-    def exchange_half(stage, step, side):
-        u = UNITS[stage]
-        start = BASES[stage] + 4 * u * side
-        at_row = start - BASES[2]
-        rows = pl.ds(at_row, 4 * u)
-        if step == 0:
-            src, partner = own.at[pl.ds(start, 4 * u)], partners[side]
-        else:
-            src, partner = pair_sum.at[rows], partners[1 - side]
-        return across(src, pair_got.at[step].at[rows], stage, step, side, partner)
-
-    def advance_doubling(stage, step):
-        u = UNITS[stage]
-        for side in range(2):
-            start = BASES[stage] + 4 * u * side
-            at_row = start - BASES[2]
+            start, end = SIDES[stage][side : side + 2]
             if step > 0:
                 exchange_half(stage, step - 1, side).wait()
-                theirs = pair_got[step - 1, at_row : at_row + 4 * u, :].astype(F32)
-            if step == 1:
-                mine = own[start : start + 4 * u, :].astype(F32)
-                pair_sum[at_row : at_row + 4 * u, :] = (mine + theirs).astype(BF16)
-            if step == 2:
-                mine = pair_sum[at_row : at_row + 4 * u, :].astype(F32)
-                whole[start : start + 4 * u, :] = (mine + theirs).astype(BF16)
+                mine = (own, pair_sum)[step - 1][start:end, :].astype(F32)
+                theirs = pair_got[step - 1, start:end, :].astype(F32)
+                (pair_sum, whole)[step - 1][start:end, :] = (mine + theirs).astype(BF16)
             if step < 2:
                 exchange_half(stage, step, side).start()
-
-    def slot(t):
-        for stage in reversed(range(4)) if t > 3 else range(4):
-            step = t - stage
-            if stage < 2 and 0 <= step <= 4:
-                advance(stage, step)
-            if stage >= 2 and 0 <= step <= 2:
-                advance_doubling(stage, step)
 
     def settle(pair):
         side, base = STRIPE * G, BASES[pair]
@@ -807,9 +729,10 @@
             own[base + side * tile : base + side * tile + side, :] = turned[
                 :, 128 * tile : 128 * tile + 128
             ]
-        own[base + 3 * side : base + 640, :] = jnp.zeros((640 - 3 * side, 128), BF16)
-        slot(pair)
-        if pair == 0:
+        advance(pair, 0)
+        if pair > 0:
+            advance(pair - 1, 1)
+        if pair == 1:
             dec.others(dec.receive)
             total = dec_got[0]
             for j in range(1, BRICKS):
@@ -821,7 +744,7 @@
             for d, peer in enumerate(x_peers):
                 small_copy(d, peer).start()
             small_got[x] = small_sent[...]
-        if pair == 1:
+        if pair == 2:
             for d, peer in enumerate(x_peers):
                 small_copy(d, peer).wait()
             small = (small_got[0] + small_got[1]) + (small_got[2] + small_got[3])
@@ -855,7 +778,8 @@
         (column >= 2 * G) & (column < 3 * G), acc_lines[2 * COMP :, :], diagonal
     )
     own[base + VM + HID + FEAT :, :] = diagonal.astype(BF16)
-    slot(3)
+    advance(3, 0)
+    advance(2, 1)
     head_sent[...] = jnp.broadcast_to(acc_out[FEAT : FEAT + 1, :], (8, 128))
 
     def head_copy(d, peer):
@@ -873,9 +797,11 @@
     head_got[x] = head_sent[...]
     for exchange in (pos, msg):
         exchange.sends_done()
-    slot(4)
+    advance(0, 2)
     settle(0)
-    settle(2)
+    advance(3, 1)
+    advance(1, 2)
+    settle(1)
     dec.others(lambda peer: spread_copy(peer, peer).wait_recv())
     decoder_sums[...] = dec_all[...]
     dec.others(lambda peer: spread_copy(peer, me).wait_send())
@@ -884,8 +810,9 @@
     for d, peer in enumerate(x_peers):
         head_copy(d, peer).wait()
     small_sums[8:16] = (head_got[0] + head_got[1]) + (head_got[2] + head_got[3])
-    slot(5)
-    settle(1)
+    advance(2, 2)
+    settle(2)
+    advance(3, 2)
     layers_out[...] = whole[BASES[3] :, :]
 
 
@@ -987,16 +914,13 @@
         ]
         + [
             vmem((PACK, 128), BF16),
-            vmem((BASES[2] // 2, 128), BF16),
-            vmem((BASES[2] // 2, 128), BF16),
-            vmem((BASES[2] // 4, 128), BF16),
             vmem((PACK, 128), BF16),
-            vmem((2, PACK - BASES[2], 128), BF16),
-            vmem((PACK - BASES[2], 128), BF16),
+            vmem((2, PACK, 128), BF16),
+            vmem((PACK, 128), BF16),
         ]
         + [dma((BRICKS,))] * 10
         + [dma((BATCH - 1,))] * 4
-        + [dma((32,))] * 2,
+        + [dma((16,))] * 2,
         compiler_params=pltpu.CompilerParams(collective_id=0, has_side_effects=True),
         name="train",
     )(

time: 76 us -> 71.1 us (0.936)
  Pallas kernels: 74.5 us -> 69.6 us
    pallas_call x1, Pallas kernels: 72.2 us -> 67.3 us  [on_device(): pl.pallas_call(train, out_shape=(shape((VM, G * G), BF16), shape((PACK -...]
where the time goes in v3:
time: 71.1 us; the launch traced here: 70.9 us
  Pallas kernels  69.6 us (98%)
  between operations  1.3 us (2%)
    pallas_call x1, Pallas kernels, on_device(): pl.pallas_call(train, out_shape=(shape((VM, G * G), BF16), shape((PACK -...  67.3 us
    pallas_call x1, Pallas kernels, on_device(): pl.pallas_call(unpack, out_shape=(shape((1, VM, G * G)), shape((1, G, VM)...  2.3 us

profile of v3, /device:TPU:0, one launch (start us, length us, event | category | flops | bytes accessed | tf_op | source)
XLA Modules:
  0.0 70.9 jit_solution(12891359504030350191)
XLA Ops:
  1.3 67.3 %train.1 = (bf16[144,1600]{1,0:T(8,128)(2,1)}, bf16[384,128]{1,0:T(8,128)(2,1)}, f32[32,8,128]{2,1,0:T(8,128)}, f32[16,128]{1,0:T(8,128)}) custom-call(s32[8,128]{1,0:T(8,128)} %bitcast.9, s32[3,8,4,128]{3,2,1,0:T(4,128)} %lattice.1, f32[3,8,4,128]{3,2,1,0:T(4,128)} %offsets.1, f32[3,128]{1,0:T(4,128)} %target.1, bf16[1,144,1600]{2,1,0:T(8,128)(2,1)} %bitcast.7, ...), custom_call_target="tpu_custom_call" | custom-call | tf_op jit(solution)/shard_map/train/pallas_call | solution.py:878
  68.6 2.3 %unpack.1 = (f32[1,144,1600]{2,1,0:T(8,128)}, f32[1,40,144]{2,1,0:T(8,128)}, f32[1,144,128]{2,1,0:T(8,128)}, f32[1,128,128]{2,1,0:T(8,128)}, f32[1,64,128]{2,1,0...) custom-call(bf16[144,1600]{1,0:T(8,128)(2,1)} %get-tuple-element.24., ...), custom_call_target="tpu_custom_call" | custom-call | tf_op jit(solution)/shard_map/unpack/pallas_call | solution.py:941
